TPU v7x, 512 devices: a whole 4x4x16 slice. The times are simulated.
512 devices in a mesh: group: 16 (over x, z_hi), shard: 32 (over z_lo, y, core).
Axes of the slice: x: 4, y: 4, z: 16 (z_hi: 4, z_lo: 4; z = z_hi * 4 + z_lo), core: 2. Of those that a mesh axis runs over, the one named last changes fastest.
Arguments:
- step_count: int32 [1], replicated, may hold values from 2 to 8
- block_order: int32 [224], replicated, may hold values from 0 to 223, as said below
- saved_tiles: bfloat16 [512, 4, 18, 18, 256], P(('group', 'shard')), may hold values from -6 to 6
- pre_act: bfloat16 [262144, 256], P(('group', 'shard')), may hold values from -6 to 6
- grad_output: bfloat16 [262144, 256], P(('group', 'shard')), may hold values from -0.0234375 to 0.0234375
- pointwise_live: bfloat16 [256, 256], replicated, may hold values from -0.375 to 0.375
- master_rows: float32 [7168, 256], P('shard'), may hold values from -0.25 to 0.25, as said below
- row_moment: float32 [7168], P('shard'), may hold values from 0.5 to 30, as said below
- col_moment: float32 [2, 256], replicated, may hold values from 0.03 to 0.3
- next_tiles: bfloat16 [512, 4, 18, 18, 256], P(('group', 'shard')), may hold values from -6 to 6
Outputs:
- update_rows: float32 [7168, 256], P('shard')
- new_master: float32 [7168, 256], P('shard')
- new_row_moment: float32 [7168], P('shard')
- new_col_moment: float32 [2, 256], replicated
- next_output: bfloat16 [262144, 256], P(('group', 'shard'))
Inputs may be any that keep to these rules, and one draw needn't show every extreme that they name: `block_order`: a permutation of 0 to 223. `master_rows`: rows of the 3x3x3 kernel are of order (6912) ** -0.5 and rows of the 1x1x1 kernel of order 256 ** -0.5. `row_moment`: positive row factors.
All inputs are finite; a program needn't handle non-finite values.
Results may differ from a plain program's by a relative error of at most 0.023.
Values may be sent and summed in bfloat16 or wider, within the bound.
A program may use at most 64 MiB of HBM per device.

v0:
```python
import jax
import jax.numpy as jnp
from jax import lax
from jax.sharding import PartitionSpec as P

CI = 256
CO = 256
BLK = 32
FR = 2
HW = 16
NB3 = 216
NB = 224
learn_rate = 0.002
decay_power = 0.8


def silu_slope(values):
    sigma = jax.nn.sigmoid(values)
    return sigma * (1.0 + values * (1.0 - sigma))


def tap_views(frames):
    views = []
    for frame_off in range(3):
        for row_off in range(3):
            for col_off in range(3):
                window = frames[
                    frame_off : frame_off + FR, row_off : row_off + HW, col_off : col_off + HW, :
                ]
                views.append(window.reshape(FR * HW * HW, CI))
    return views


def contract_rows(left, right):
    return lax.dot_general(
        left, right, (((0,), (0,)), ((), ())), preferred_element_type=jnp.float32
    )


def kernel_sums(values, is_small):
    large_part = jnp.sum(jnp.where(is_small[:, None], 0.0, values), axis=0)
    small_part = jnp.sum(jnp.where(is_small[:, None], values, 0.0), axis=0)
    return jnp.stack([large_part, small_part])


def shards(
    step_count,
    block_order,
    saved_tiles,
    pre_act,
    grad_output,
    pointwise_live,
    master_rows,
    row_moment,
    col_moment,
    next_tiles,
):
    pre_float = pre_act.astype(jnp.float32)
    activation = jax.nn.silu(pre_float).astype(jnp.bfloat16)
    grad_act = lax.dot_general(
        grad_output, pointwise_live, (((1,), (1,)), ((), ())), preferred_element_type=jnp.float32
    )
    grad_pre = (grad_act * silu_slope(pre_float)).astype(jnp.bfloat16)
    pieces = [contract_rows(view, grad_pre) for view in tap_views(saved_tiles[0])]
    pieces.append(contract_rows(activation, grad_output))
    own_term = jnp.concatenate(pieces, axis=0).astype(jnp.bfloat16)
    total_rows = NB * BLK
    stored = jnp.take(own_term.reshape(NB, BLK, CO), block_order, axis=0).reshape(total_rows, CO)
    own_rows = master_rows.shape[0]
    partial_value = lax.psum_scatter(stored, "shard", scatter_dimension=0, tiled=True).astype(
        jnp.float32
    )
    gradient = lax.psum(partial_value, "group")
    owner = lax.axis_index("shard")
    own_count = own_rows // BLK
    own_blocks = lax.dynamic_slice_in_dim(block_order, owner * own_count, own_count)
    is_small = jnp.repeat(own_blocks >= NB3, BLK, total_repeat_length=own_rows)
    decay_rate = 1.0 - step_count.astype(jnp.float32)[0] ** (-decay_power)
    counts = jnp.array([27 * CI, CO], jnp.float32)
    squares = gradient * gradient
    new_row = decay_rate * row_moment + (1.0 - decay_rate) * jnp.mean(squares, axis=1)
    col_part = kernel_sums(squares, is_small)
    row_part = kernel_sums(new_row[:, None], is_small)[:, 0]
    col_total, row_total = lax.psum((col_part, row_part), "shard")
    new_col = decay_rate * col_moment + (1.0 - decay_rate) * col_total / counts[:, None]
    row_mean = row_total / counts
    col_rows = jnp.where(is_small[:, None], new_col[1], new_col[0])
    mean_rows = jnp.where(is_small, row_mean[1], row_mean[0])
    scaled = gradient / jnp.sqrt(new_row[:, None] * col_rows / mean_rows[:, None])
    square_part = kernel_sums(jnp.sum(scaled * scaled, axis=1)[:, None], is_small)[:, 0]
    square_total = lax.psum(square_part, "shard")
    clip_factor = jnp.maximum(1.0, jnp.sqrt(square_total / (counts * CO)))
    update_rows = scaled / jnp.where(is_small, clip_factor[1], clip_factor[0])[:, None]
    new_master = master_rows - learn_rate * update_rows
    weights_low = new_master.astype(jnp.bfloat16)
    gathered = lax.all_gather(weights_low, "shard", axis=0, tiled=True)
    inverse = jnp.zeros((NB,), jnp.int32).at[block_order].set(jnp.arange(NB, dtype=jnp.int32))
    natural = jnp.take(gathered.reshape(NB, BLK, CO), inverse, axis=0).reshape(total_rows, CO)
    spatial = natural[: 27 * CI].reshape(27, CI, CO)
    pointwise = natural[27 * CI :]
    hidden_sum = jnp.zeros((FR * HW * HW, CO), jnp.float32)
    for index_tap, view in enumerate(tap_views(next_tiles[0])):
        hidden_sum = hidden_sum + jnp.dot(
            view, spatial[index_tap], preferred_element_type=jnp.float32
        )
    hidden_act = jax.nn.silu(hidden_sum).astype(jnp.bfloat16)
    next_output = jnp.dot(hidden_act, pointwise, preferred_element_type=jnp.float32).astype(
        jnp.bfloat16
    )
    return (update_rows, new_master, new_row, new_col, next_output)


def solution(mesh):
    in_specs = (
        P(),
        P(),
        P(("group", "shard"), None, None, None, None),
        P(("group", "shard"), None),
        P(("group", "shard"), None),
        P(),
        P("shard", None),
        P("shard"),
        P(),
        P(("group", "shard"), None, None, None, None),
    )
    out_specs = (P("shard", None), P("shard", None), P("shard"), P(), P(("group", "shard"), None))
    return jax.shard_map(shards, mesh=mesh, in_specs=in_specs, out_specs=out_specs, check_vma=False)
```

profile of v0, /device:TPU:1, one launch (start us, length us, event | category | flops | bytes accessed | tf_op | source)
XLA Modules:
  0.0 556.7 jit_solution(18183779678937260853)
XLA Ops:
  7.2 1.3 copy.102
  10.0 0.9 fusion.14
  11.9 0.9 fusion.18
  13.8 0.9 fusion.22
  14.7 0.9 fusion.24
  15.6 0.9 fusion.26
  16.6 0.9 fusion.28
  17.5 0.9 fusion.30
  18.5 0.9 fusion.32
  19.4 0.9 fusion.34
  20.3 0.9 fusion.36
  21.3 0.9 fusion.38
  23.1 0.9 fusion.42
  24.1 0.9 fusion.44
  25.0 0.9 fusion.46
  25.9 0.9 fusion.48
  27.8 0.9 fusion.52
  28.8 0.9 fusion.54
  29.7 0.9 fusion.56
  30.6 0.9 fusion.58
  31.6 0.9 fusion.60
  32.5 0.9 fusion.62
  35.3 1.0 fusion.12
  36.3 4.9 gather_fusion
  41.2 3.8 broadcast_select_fusion.1
  46.8 4.5 select_select_fusion
  51.3 150.8 %reduce-scatter.2.cloned.1.call-done = bf16[224,256]{1,0:T(8,128)(2,1)} async-done(((bf16[7168,256]{1,0:T(8,128)(2,1)}), bf16[224,256]{1,0:T(8,128)(2,1)}) %reduce-scatter.2.cloned.1.call-update) | async-done | bytes 114704 | tf_op jit(solution)/shard_map/reduce_scatter | solution.py:70
  202.1 89.2 %all-reduce.2 = f32[224,256]{1,0:T(8,128)S(1)} all-reduce(bf16[224,256]{1,0:T(8,128)(2,1)} %reduce-scatter.2.cloned.1.call-done), channel_id=1, replica_groups=mesh['group'=16,'shard'=32] {'group'}, use_global_device_ids=true, to_apply=%region_1.3 | all-reduce | flops 57344 | bytes 344064 | tf_op jit(solution)/shard_map/psum | solution.py:73
  291.5 5.2 select_reduce_fusion.5
  296.7 1.3 maximum_bitcast_fusion
  298.0 84.7 %all-reduce = (f32[2]{0:T(128)S(1)}, f32[2,256]{1,0:T(2,128)S(1)}) all-reduce(f32[2]{0:T(128)S(1)} %maximum_bitcast_fusion, f32[2,256]{1,0:T(2,128)S(1)} %pad_maximum_fusion), channel_id=1, replica_groups=mesh['group'=16,'shard'=32] {'shard'}, use_global_device_ids=true, to_apply=%region_8.10 | all-reduce | flops 514 | bytes 4112 | tf_op jit(solution)/shard_map/psum | solution.py:84
  383.3 5.7 %broadcast_select_fusion.3 = f32[224]{0:T(256)S(1)} fusion(f32[]{:T(128)} %bitcast.74, f32[]{:T(128)} %bitcast.73, pred[]{:T(512)} %bitcast.65, pred[]{:T(512)} %bitcast.64, pred[]{:T(512)} %bitcast.63, pred[]{:T(512)} %bitcast.62, pred[]{:T(512)} %bitcast.61, pred[]{:T(512)} %bitcast.60, pred[]{:T(512)} %bitcast.59, s32[256]{0:T(256)S(1)} %add_bitcast_fusion), kind=kLoop, calls=%fused_computation.172 | loop fusion | flops 4704 | bytes 1807 | tf_op jit(solution)/shard_map/jit(_where)/select_n | solution.py:88
  389.3 5.2 select_reduce_fusion.3
  394.5 1.3 maximum_bitcast_fusion.1
  395.8 67.4 %psum.31 = f32[2]{0:T(128)S(1)} all-reduce(f32[2]{0:T(128)S(1)} %maximum_bitcast_fusion.1), channel_id=1, replica_groups=mesh['group'=16,'shard'=32] {'shard'}, use_global_device_ids=true, to_apply=%region_12.14 | all-reduce | flops 2 | bytes 16 | tf_op jit(solution)/shard_map/psum | solution.py:91
  463.8 5.7 %broadcast_select_fusion.2 = f32[224]{0:T(256)S(1)} fusion(f32[]{:T(128)} %bitcast.79, f32[]{:T(128)} %bitcast.78, pred[]{:T(512)} %bitcast.65, pred[]{:T(512)} %bitcast.64, pred[]{:T(512)} %bitcast.63, pred[]{:T(512)} %bitcast.62, pred[]{:T(512)} %bitcast.61, pred[]{:T(512)} %bitcast.60, pred[]{:T(512)} %bitcast.59, s32[256]{0:T(256)S(1)} %add_bitcast_fusion), kind=kLoop, calls=%fused_computation.171 | loop fusion | flops 4704 | bytes 1807 | tf_op jit(solution)/shard_map/jit(_where)/select_n | solution.py:93
  470.5 1.5 scatter_custom_fusion
  472.1 1.4 fusion.85
  473.5 2.1 fusion.84
  475.6 53.3 %all-gather.2.cloned.1.call-done = bf16[7168,256]{1,0:T(8,128)(2,1)} async-done(((bf16[224,256]{1,0:T(8,128)(2,1)}), bf16[7168,256]{1,0:T(8,128)(2,1)}) %all-gather.2.cloned.1.call-update) | async-done | bytes 3670032 | tf_op jit(solution)/shard_map/all_gather | solution.py:96
  528.9 4.9 gather_fusion.1
  533.8 2.5 broadcast_select_fusion
  536.4 1.0 fusion.82
  539.0 1.0 convolution_bitcast_fusion.6
  540.1 1.0 convolution_bitcast_fusion.7
  541.1 1.1 convolution_bitcast_fusion.8
  545.9 1.1 fusion.10
  547.0 2.9 convolution_convert_fusion
  (124 shorter events, 15.9 us)
Async XLA Ops:
  7.2 2.3 copy-start
  7.2 194.9 %reduce-scatter.2.cloned.1.call-start = ((), (), s32[]{:S(2)}) async-start(), calls=%async_computation.1 | async-start | bytes 3784704 | tf_op jit(solution)/shard_map/reduce_scatter | solution.py:70
  8.7 0.7 copy-start.27
  8.7 1.0 copy-start.30
  8.7 1.0 copy-start.31
  45.0 1.8 copy-start.28
  45.0 246.5 %copy-start.26 = (f32[224]{0:T(256)S(1)}, f32[224]{0:T(256)}, u32[]{:S(2)}) copy-start(f32[224]{0:T(256)} %param.22) | copy-start | bytes 2692
  45.0 337.7 %copy-start.25 = (f32[2,256]{1,0:T(2,128)S(1)}, f32[2,256]{1,0:T(2,128)}, u32[]{:S(2)}) copy-start(f32[2,256]{1,0:T(2,128)} %param.23) | copy-start | bytes 6148
  45.0 337.7 %copy-start.29 = (f32[2]{0:T(128)S(1)}, f32[2]{0:T(128)}, u32[]{:S(2)}) copy-start(f32[2]{0:T(128)} %constant.126) | copy-start | bytes 28
  45.0 418.2 %copy-start.32 = (f32[2]{0:T(128)S(1)}, f32[2]{0:T(128)}, u32[]{:S(2)}) copy-start(f32[2]{0:T(128)} %constant.129) | copy-start | bytes 28
  45.0 424.5 %copy-start.22 = (f32[224,256]{1,0:T(8,128)S(1)}, f32[224,256]{1,0:T(8,128)}, u32[]{:S(2)}) copy-start(f32[224,256]{1,0:T(8,128)} %param.21) | copy-start | bytes 688132
  45.0 426.9 %copy-start.21 = (bf16[1,4,18,18,256]{4,1,3,2,0:T(4,128)(2,1)S(1)}, bf16[1,4,18,18,256]{4,1,3,2,0:T(4,128)(2,1)}, u32[]{:S(2)}) copy-start(bf16[1,4,18,18,256]{4,1,3,2,0:T(4,128)(2,1)} %param.24) | copy-start | bytes 1990660
  45.0 483.9 %all-gather.2.cloned.1.call-start = ((), (), s32[]{:S(2)}) async-start(), calls=%async_computation.2 | async-start | bytes 3784704 | tf_op jit(solution)/shard_map/all_gather | solution.py:96
  296.7 176.9 %copy-start.24 = (f32[224]{0:T(256)}, f32[224]{0:T(256)S(1)}, u32[]{:S(2)}) copy-start(f32[224]{0:T(256)S(1)} %get-tuple-element.32) | copy-start | bytes 2692
  382.7 90.8 %copy-start.23 = (f32[2,256]{1,0:T(2,128)}, f32[2,256]{1,0:T(2,128)S(1)}, u32[]{:S(2)}) copy-start(f32[2,256]{1,0:T(2,128)S(1)} %multiply_add_fusion) | copy-start | bytes 6148
  537.4 1.4 copy-start.4
  537.4 1.7 copy-start.3
  537.4 2.7 copy-start.2
  537.6 3.5 copy-start.1
  537.8 4.3 copy-start.20
  538.3 4.1 copy-start.19
  538.5 4.1 copy-start.18
  539.0 3.9 copy-start.17
  540.1 3.1 copy-start.16
  542.2 1.3 copy-start.14
  542.4 1.3 copy-start.12
  542.6 1.3 copy-start.15
  542.9 1.3 copy-start.13
  543.2 1.3 copy-start.11
  543.4 1.3 copy-start.10
  543.7 1.3 copy-start.9
  543.9 1.3 copy-start.8
  544.2 1.2 copy-start.7
  544.4 1.2 copy-start.6
  544.7 1.2 copy-start.5
Sparse Core Ops, SparseCore 0:
  45.2 156.8 reduce-scatter.1
  470.6 58.3 all-gather.1
where the time goes:
time: 557 us
  blocking collectives  241 us (43%)
  waiting for transfers between devices  204 us (37%)
  matrix products  38.5 us (7%)
  other arithmetic  36.8 us (7%)
  local copies, waits for them, and re-layouts  20.3 us (4%)
  between operations  15.6 us (3%)
    reduce_scatter x1, waiting for transfers between devices, shards(): lax.psum_scatter(stored, 'shard', scatter_dimension=0, tiled=True)  151 us
    psum x1, blocking collectives, shards(): gradient = lax.psum(partial_value, 'group')  89.2 us
    psum x1, blocking collectives, shards(): col_total, row_total = lax.psum((col_part, row_part), 'shard')  84.7 us
    psum x1, blocking collectives, shards(): square_total = lax.psum(square_part, 'shard')  67.4 us
    all_gather x1, waiting for transfers between devices, shards(): gathered = lax.all_gather(weights_low, 'shard', axis=0, tiled=True)  53.3 us
    dot_general x28, matrix products, contract_rows(): lax.dot_general(left, right, (((0,), (0,)), ((), ())), preferred_element_...  26.2 us
  transfers between devices with their start and end apart: 2, of which 2 were waited for; matrix products, arithmetic and copies ran while one was open for 2% of the time, Pallas kernels for 0%

commit v1 on v0

--- a/solution.py
+++ b/solution.py
@@ -93,7 +93,10 @@
     update_rows = scaled / jnp.where(is_small, clip_factor[1], clip_factor[0])[:, None]
     new_master = master_rows - learn_rate * update_rows
     weights_low = new_master.astype(jnp.bfloat16)
-    gathered = lax.all_gather(weights_low, "shard", axis=0, tiled=True)
+    count = lax.axis_size("shard")
+    blocks = jnp.stack([weights_low for _ in range(count)])
+    blocks = lax.all_to_all(blocks, "shard", split_axis=0, concat_axis=0)
+    gathered = jnp.concatenate(blocks, axis=0)
     inverse = jnp.zeros((NB,), jnp.int32).at[block_order].set(jnp.arange(NB, dtype=jnp.int32))
     natural = jnp.take(gathered.reshape(NB, BLK, CO), inverse, axis=0).reshape(total_rows, CO)
     spatial = natural[: 27 * CI].reshape(27, CI, CO)

time: 557 us -> 586 us (1.052)
  waiting for transfers between devices: 204 us -> 228 us
    all_to_all x0 -> x1, waiting for transfers between devices: none -> 76.8 us  [shards(): blocks = lax.all_to_all(blocks, 'shard', split_axis=0, concat_axis=0)]
    all_gather x1 -> x0, waiting for transfers between devices: 53.3 us -> none  [shards(): gathered = lax.all_gather(weights_low, 'shard', axis=0, tiled=True)]
where the time goes in v1:
time: 586 us
  blocking collectives  240 us (41%)
  waiting for transfers between devices  228 us (39%)
  matrix products  38.7 us (7%)
  other arithmetic  36.2 us (6%)
  local copies, waits for them, and re-layouts  22.6 us (4%)
  between operations  15.5 us (3%)
    reduce_scatter x1, waiting for transfers between devices, shards(): lax.psum_scatter(stored, 'shard', scatter_dimension=0, tiled=True)  151 us
    psum x1, blocking collectives, shards(): gradient = lax.psum(partial_value, 'group')  88.5 us
    psum x1, blocking collectives, shards(): col_total, row_total = lax.psum((col_part, row_part), 'shard')  83.9 us
    all_to_all x1, waiting for transfers between devices, shards(): blocks = lax.all_to_all(blocks, 'shard', split_axis=0, concat_axis=0)  76.8 us
    psum x1, blocking collectives, shards(): square_total = lax.psum(square_part, 'shard')  67.4 us
    dot_general x28, matrix products, contract_rows(): lax.dot_general(left, right, (((0,), (0,)), ((), ())), preferred_element_...  26.4 us
  transfers between devices with their start and end apart: 2, of which 2 were waited for; matrix products, arithmetic and copies ran while one was open for 2% of the time, Pallas kernels for 0%

profile of v1, /device:TPU:1, one launch (start us, length us, event | category | flops | bytes accessed | tf_op | source)
XLA Modules:
  0.0 585.7 jit_solution(4013844934246655540)
XLA Ops:
  7.2 1.3 copy.102
  10.0 0.9 fusion.14
  11.9 0.9 fusion.18
  12.9 0.9 fusion.20
  13.8 0.9 fusion.22
  14.7 0.9 fusion.24
  15.7 0.9 fusion.26
  16.6 0.9 fusion.28
  17.6 0.9 fusion.30
  18.5 0.9 fusion.32
  20.4 0.9 fusion.36
  22.3 0.9 fusion.40
  23.2 1.0 fusion.42
  24.2 0.9 fusion.44
  25.1 0.9 fusion.46
  26.0 0.9 fusion.48
  29.8 1.0 fusion.56
  32.6 1.0 fusion.62
  33.5 0.9 fusion.64
  34.5 0.9 fusion.66
  35.4 1.0 fusion.12
  36.4 4.9 gather_fusion
  41.3 3.8 broadcast_select_fusion.1
  46.8 4.5 select_select_fusion
  51.2 151.0 %reduce-scatter.2.cloned.1.call-done = bf16[224,256]{1,0:T(8,128)(2,1)} async-done(((bf16[7168,256]{1,0:T(8,128)(2,1)}), bf16[224,256]{1,0:T(8,128)(2,1)}) %reduce-scatter.2.cloned.1.call-update) | async-done | bytes 114704 | tf_op jit(solution)/shard_map/reduce_scatter | solution.py:70
  202.2 88.5 %all-reduce.2 = f32[224,256]{1,0:T(8,128)S(1)} all-reduce(bf16[224,256]{1,0:T(8,128)(2,1)} %reduce-scatter.2.cloned.1.call-done), channel_id=1, replica_groups=mesh['group'=16,'shard'=32] {'group'}, use_global_device_ids=true, to_apply=%region_1.3 | all-reduce | flops 57344 | bytes 344064 | tf_op jit(solution)/shard_map/psum | solution.py:73
  290.9 5.1 select_reduce_fusion.5
  296.0 1.3 maximum_bitcast_fusion
  297.2 83.9 %all-reduce = (f32[2]{0:T(128)S(1)}, f32[2,256]{1,0:T(2,128)S(1)}) all-reduce(f32[2]{0:T(128)S(1)} %maximum_bitcast_fusion, f32[2,256]{1,0:T(2,128)S(1)} %pad_maximum_fusion), channel_id=1, replica_groups=mesh['group'=16,'shard'=32] {'shard'}, use_global_device_ids=true, to_apply=%region_8.10 | all-reduce | flops 514 | bytes 4112 | tf_op jit(solution)/shard_map/psum | solution.py:84
  381.8 5.6 broadcast_select_fusion.3
  387.7 5.1 select_reduce_fusion.3
  392.8 1.3 maximum_bitcast_fusion.1
  394.0 67.4 %psum.31 = f32[2]{0:T(128)S(1)} all-reduce(f32[2]{0:T(128)S(1)} %maximum_bitcast_fusion.1), channel_id=1, replica_groups=mesh['group'=16,'shard'=32] {'shard'}, use_global_device_ids=true, to_apply=%region_12.14 | all-reduce | flops 2 | bytes 16 | tf_op jit(solution)/shard_map/psum | solution.py:91
  462.0 5.6 broadcast_select_fusion.2
  468.5 2.3 stack.29
  470.8 5.2 all-to-all-start
  476.0 1.5 scatter_custom_fusion
  477.7 1.4 fusion.85
  479.1 2.1 fusion.84
  481.2 76.8 %all-to-all-done = bf16[32,224,256]{2,1,0:T(8,128)(2,1)} async-done(((bf16[32,224,256]{2,1,0:T(8,128)(2,1)}), bf16[32,224,256]{2,1,0:T(8,128)(2,1)}, u32[]{:S(2)}, u32[]{:S(2)}) %all-to-all-start) | async-done | bytes 3670048 | tf_op jit(solution)/shard_map/all_to_all | solution.py:98
  557.9 4.9 gather_fusion.1
  562.8 2.5 broadcast_select_fusion
  565.4 1.0 fusion.82
  568.0 1.0 convolution_bitcast_fusion.6
  569.1 1.0 convolution_bitcast_fusion.7
  570.1 1.1 convolution_bitcast_fusion.8
  574.9 1.1 fusion.10
  576.0 2.9 convolution_convert_fusion
  (124 shorter events, 17.7 us)
Async XLA Ops:
  7.2 2.3 copy-start
  7.2 195.0 %reduce-scatter.2.cloned.1.call-start = ((), (), s32[]{:S(2)}) async-start(), calls=%async_computation.2 | async-start | bytes 3784704 | tf_op jit(solution)/shard_map/reduce_scatter | solution.py:70
  8.7 0.7 copy-start.27
  8.7 1.0 copy-start.30
  8.7 1.0 copy-start.31
  45.1 1.6 copy-start.28
  45.1 245.8 %copy-start.26 = (f32[224]{0:T(256)S(1)}, f32[224]{0:T(256)}, u32[]{:S(2)}) copy-start(f32[224]{0:T(256)} %param.22) | copy-start | bytes 2692
  45.1 336.0 %copy-start.25 = (f32[2,256]{1,0:T(2,128)S(1)}, f32[2,256]{1,0:T(2,128)}, u32[]{:S(2)}) copy-start(f32[2,256]{1,0:T(2,128)} %param.23) | copy-start | bytes 6148
  45.1 336.0 %copy-start.29 = (f32[2]{0:T(128)S(1)}, f32[2]{0:T(128)}, u32[]{:S(2)}) copy-start(f32[2]{0:T(128)} %constant.126) | copy-start | bytes 28
  45.1 416.3 %copy-start.32 = (f32[2]{0:T(128)S(1)}, f32[2]{0:T(128)}, u32[]{:S(2)}) copy-start(f32[2]{0:T(128)} %constant.129) | copy-start | bytes 28
  45.1 422.6 %copy-start.22 = (f32[224,256]{1,0:T(8,128)S(1)}, f32[224,256]{1,0:T(8,128)}, u32[]{:S(2)}) copy-start(f32[224,256]{1,0:T(8,128)} %param.21) | copy-start | bytes 688132
  296.0 174.8 %copy-start.24 = (f32[224]{0:T(256)}, f32[224]{0:T(256)S(1)}, u32[]{:S(2)}) copy-start(f32[224]{0:T(256)S(1)} %get-tuple-element.32) | copy-start | bytes 2692
  381.2 89.6 %copy-start.23 = (f32[2,256]{1,0:T(2,128)}, f32[2,256]{1,0:T(2,128)S(1)}, u32[]{:S(2)}) copy-start(f32[2,256]{1,0:T(2,128)S(1)} %multiply_add_fusion) | copy-start | bytes 6148
  470.8 6.7 %copy-start.21 = (bf16[1,4,18,18,256]{4,1,3,2,0:T(4,128)(2,1)S(1)}, bf16[1,4,18,18,256]{4,1,3,2,0:T(4,128)(2,1)}, u32[]{:S(2)}) copy-start(bf16[1,4,18,18,256]{4,1,3,2,0:T(4,128)(2,1)} %param.24) | copy-start | bytes 1990660
  470.8 87.1 %all-to-all-start = ((bf16[32,224,256]{2,1,0:T(8,128)(2,1)}), bf16[32,224,256]{2,1,0:T(8,128)(2,1)}, u32[]{:S(2)}, u32[]{:S(2)}) async-start(bf16[32,224,256]{2,1,0:T(8,128)(2,1)} %stack.29), calls=%async_computation.1 | async-start | bytes 7340032 | tf_op jit(solution)/shard_map/all_to_all | solution.py:98
  566.4 1.4 copy-start.4
  566.4 1.7 copy-start.3
  566.4 2.7 copy-start.2
  566.6 3.5 copy-start.1
  566.8 4.3 copy-start.20
  567.3 4.1 copy-start.19
  567.5 4.1 copy-start.18
  568.0 3.9 copy-start.17
  569.1 3.1 copy-start.16
  571.2 1.3 copy-start.14
  571.4 1.3 copy-start.12
  571.6 1.3 copy-start.15
  571.9 1.3 copy-start.13
  572.1 1.3 copy-start.11
  572.4 1.3 copy-start.10
  572.7 1.3 copy-start.9
  572.9 1.3 copy-start.8
  573.2 1.2 copy-start.7
  573.4 1.2 copy-start.6
  573.7 1.2 copy-start.5
Sparse Core Ops, SparseCore 0:
  45.2 156.8 reduce-scatter.1
